TPU v7x, 256 devices: a whole 4x4x8 slice. The times are simulated.
256 devices in a mesh: span: 16 (over z, x_hi), sp: 8 (over y, x_lo), fsdp: 2 (over core).
Axes of the slice: x: 4 (x_hi: 2, x_lo: 2; x = x_hi * 2 + x_lo), y: 4, z: 8, core: 2. Of those that a mesh axis runs over, the one named last changes fastest.
Arguments:
- query_pre: bfloat16 [2, 16384, 3072], P('fsdp', ('span', 'sp')), may hold values from -12 to 12
- key_pre: bfloat16 [2, 16384, 3072], P('fsdp', ('span', 'sp')), may hold values from -12 to 12
- values: bfloat16 [2, 16384, 3072], P('fsdp', ('span', 'sp')), may hold values from -6 to 6
- cotangent: bfloat16 [2, 16384, 3072], P('fsdp', ('span', 'sp')), may hold values from -6 to 6
- gains: float32 [2, 3072], P(None, 'fsdp'), may hold values from 0.5 to 1.5
- frame_span: int32 [2, 16384], P('fsdp', 'span'), may hold values from 0 to 31, as said below
- denoise_steps: int32 [2, 32], P('fsdp'), may hold values from 1 to 4
Outputs:
- query_grad: bfloat16 [2, 16384, 3072], P('fsdp', ('span', 'sp'))
- key_grad: bfloat16 [2, 16384, 3072], P('fsdp', ('span', 'sp'))
- value_grad: bfloat16 [2, 16384, 3072], P('fsdp', ('span', 'sp'))
- gain_grad: float32 [2, 3072], P(None, 'fsdp')
Inputs may be any that keep to these rules, and one draw needn't show every extreme that they name: `frame_span`: never falls along a video. Group g (tokens g * 1024 to (g + 1) * 1024 - 1) holds frame spans 2 g and 2 g + 1, each from a quarter to three quarters of the group's tokens.
All inputs are finite; a program needn't handle non-finite values.
Results may differ from a plain program's by a relative error of at most 0.0081.
The roundings to bfloat16 on the way count: a program that leaves them out, or rounds other values in their place, can miss the bound.
Values may be sent and summed in bfloat16 or wider, within the bound.
No kernel may reach another device: no remote copies, remote signals or barrier semaphores. Data moves between devices by JAX's collectives and lax.ppermute only.
A program may use at most 128 MiB of HBM per device.

v0:
```python
import jax
import jax.numpy as jnp
from jax import lax
from jax.sharding import PartitionSpec as P

HDIM = 128
EPSILON = 1e-06
NEGATIVE = -1e30


def from_behind(value, axis, steps):
    count = lax.axis_size(axis)
    first, last = (max(0, -steps), min(count, count - steps))
    return lax.ppermute(value, axis, [(source, source + steps) for source in range(first, last)])


def normed(raw_rows, gain_row):
    wide = raw_rows.astype(jnp.float32)
    inverse_rms = lax.rsqrt(jnp.mean(wide * wide, axis=-1, keepdims=True) + EPSILON)
    normal_rows = wide * inverse_rms
    return (normal_rows, inverse_rms, (normal_rows * gain_row).astype(jnp.bfloat16))


def norm_backward(grad_rows, normal_rows, inverse_rms, gain_row):
    upstream = grad_rows.astype(jnp.float32)
    scaled = upstream * gain_row
    inner = jnp.mean(scaled * normal_rows, axis=-1, keepdims=True)
    result = (inverse_rms * (scaled - normal_rows * inner)).astype(jnp.bfloat16)
    return (result, jnp.sum(upstream * normal_rows, axis=0))


def across(left, right):
    return lax.dot_general(
        left, right, (((1,), (1,)), ((), ())), preferred_element_type=jnp.float32
    )


def downward(left, right):
    return lax.dot_general(
        left, right, (((0,), (0,)), ((), ())), preferred_element_type=jnp.float32
    )


def head_grads(
    query_head, grad_head, key_joined, value_joined, joined_mask, step_weight, own_width
):
    score_scale = HDIM ** (-0.5)
    scores = across(query_head, key_joined) * score_scale
    masked = jnp.where(joined_mask, scores, NEGATIVE)
    row_max = jnp.max(masked, axis=1)
    row_total = jnp.sum(jnp.exp(masked - row_max[:, None]), axis=1)
    log_total = row_max + jnp.log(row_total)
    grad_prob = across(grad_head, value_joined)
    probs = jnp.where(joined_mask, jnp.exp(scores - log_total[:, None]), 0.0)
    row_delta = jnp.sum(probs * grad_prob, axis=1)
    factor = step_weight[:, None]
    sgrad = (factor * probs * (grad_prob - row_delta[:, None])).astype(jnp.bfloat16)
    weights = (factor * probs).astype(jnp.bfloat16)
    query_part = jnp.dot(sgrad, key_joined, preferred_element_type=jnp.float32) * score_scale
    key_own_grad = downward(sgrad[:, :own_width], query_head) * score_scale
    value_own_grad = downward(weights[:, :own_width], grad_head)
    return (
        query_part,
        key_own_grad,
        value_own_grad,
        sgrad[:, own_width:],
        weights[:, own_width:],
        log_total,
        row_delta,
    )


def on_device(query_pre, key_pre, values, cotangent, gains, frame_span, denoise_steps):
    gain_full = lax.all_gather(gains, "fsdp", axis=1, tiled=True)
    q_normal, q_inverse, q_ready = normed(query_pre[0], gain_full[0])
    k_normal, k_inverse, k_ready = normed(key_pre[0], gain_full[1])
    heads_query, heads_key, heads_value, heads_grad = (
        lax.all_to_all(q_ready, "sp", split_axis=1, concat_axis=0, tiled=True),
        lax.all_to_all(k_ready, "sp", split_axis=1, concat_axis=0, tiled=True),
        lax.all_to_all(values[0], "sp", split_axis=1, concat_axis=0, tiled=True),
        lax.all_to_all(cotangent[0], "sp", split_axis=1, concat_axis=0, tiled=True),
    )
    head_count = heads_query.shape[1] // HDIM
    own_width = heads_query.shape[0]
    span_ids = frame_span[0]
    step_table = denoise_steps[0].astype(jnp.float32)
    matches = span_ids[:, None] == lax.iota(jnp.int32, step_table.shape[0])[None, :]
    step_weight = jnp.sum(jnp.where(matches, step_table[None, :], 0.0), axis=1)
    group_index = lax.axis_index("span")
    key_prev, value_prev = from_behind((heads_key, heads_value), "span", 1)
    own_mask = span_ids[None, :] <= span_ids[:, None]
    prev_open = group_index > 0
    prev_mask = jnp.broadcast_to(prev_open, own_mask.shape)
    joined_mask = jnp.concatenate([own_mask, prev_mask], axis=1)
    key_joined_all = jnp.concatenate([heads_key, key_prev], axis=0)
    value_joined_all = jnp.concatenate([heads_value, value_prev], axis=0)
    query_parts = []
    key_parts = []
    value_parts = []
    sgrad_list = []
    weight_list = []
    total_list = []
    delta_list = []
    for head_index in range(head_count):
        first = head_index * HDIM
        last = first + HDIM
        outcome = head_grads(
            heads_query[:, first:last],
            heads_grad[:, first:last],
            key_joined_all[:, first:last],
            value_joined_all[:, first:last],
            joined_mask,
            step_weight,
            own_width,
        )
        query_parts.append(outcome[0])
        key_parts.append(outcome[1])
        value_parts.append(outcome[2])
        sgrad_list.append(outcome[3])
        weight_list.append(outcome[4])
        total_list.append(outcome[5])
        delta_list.append(outcome[6])
    query_attn = jnp.concatenate(query_parts, axis=1)
    key_own = jnp.concatenate(key_parts, axis=1)
    value_own = jnp.concatenate(value_parts, axis=1)
    key_terms = []
    value_terms = []
    for head_index in range(head_count):
        first = head_index * HDIM
        last = first + HDIM
        key_terms.append(
            downward(sgrad_list[head_index], heads_query[:, first:last]) * HDIM ** (-0.5)
        )
        value_terms.append(downward(weight_list[head_index], heads_grad[:, first:last]))
    key_back, value_back = from_behind(
        (jnp.concatenate(key_terms, axis=1), jnp.concatenate(value_terms, axis=1)), "span", -1
    )
    key_attn = key_own + key_back
    value_attn = value_own + value_back
    query_tokens, key_tokens, value_tokens = (
        lax.all_to_all(
            query_attn.astype(jnp.bfloat16), "sp", split_axis=0, concat_axis=1, tiled=True
        ),
        lax.all_to_all(
            key_attn.astype(jnp.bfloat16), "sp", split_axis=0, concat_axis=1, tiled=True
        ),
        lax.all_to_all(
            value_attn.astype(jnp.bfloat16), "sp", split_axis=0, concat_axis=1, tiled=True
        ),
    )
    query_back, query_gain = norm_backward(query_tokens, q_normal, q_inverse, gain_full[0])
    key_back_rows, key_gain = norm_backward(key_tokens, k_normal, k_inverse, gain_full[1])
    partial_value = jnp.stack([query_gain, key_gain])
    summed = lax.psum(partial_value, ("span", "sp"))
    gain_grad = lax.psum_scatter(summed, "fsdp", scatter_dimension=1, tiled=True)
    return (query_back[None], key_back_rows[None], value_tokens[None], gain_grad)


def solution(mesh):
    placed = (
        P("fsdp", ("span", "sp"), None),
        P("fsdp", ("span", "sp"), None),
        P("fsdp", ("span", "sp"), None),
        P("fsdp", ("span", "sp"), None),
        P(None, "fsdp"),
        P("fsdp", "span"),
        P("fsdp", None),
    )
    return jax.shard_map(
        on_device,
        mesh=mesh,
        in_specs=placed,
        out_specs=(
            P("fsdp", ("span", "sp"), None),
            P("fsdp", ("span", "sp"), None),
            P("fsdp", ("span", "sp"), None),
            P(None, "fsdp"),
        ),
        check_vma=False,
    )
```

profile of v0, /device:TPU:0, one launch (start us, length us, event | category | flops | bytes accessed | tf_op | source)
XLA Modules:
  0.0 1031.0 jit_solution(12937883028764885410)
XLA Ops:
  7.2 2.4 copy.78
  9.5 4.2 all-to-all-start.2
  18.8 7.4 all-to-all-done.2
  26.2 3.5 all-to-all-start.1
  29.8 2.3 copy.80
  32.1 9.4 all-to-all-done.1
  41.5 4.3 all-to-all-start.3
  46.3 5.9 collective-permute-start
  53.5 6.6 all-to-all-done.3
  60.1 4.2 all-to-all-start
  65.1 2.3 copy.79
  67.4 2.3 copy.81
  69.7 2.9 collective-permute-start.1
  72.6 12.8 %all-to-all-done = bf16[128,8,384]{2,0,1:T(8,128)(2,1)} async-done(((bf16[128,8,384]{2,0,1:T(8,128)(2,1)}), bf16[128,8,384]{2,0,1:T(8,128)(2,1)}, u32[]{:S(2)}, u32[]{:S(2)}) %all-to-all-start) | async-done | bytes 786464 | tf_op jit(solution)/shard_map/all_to_all | solution.py:78
  85.4 2.3 fusion.75
  87.7 2.7 fusion.82
  90.4 9.0 fusion.9
  99.4 8.6 exponential_reduce_fusion.2
  108.0 5.4 fusion.68
  113.4 5.4 fusion.61
  118.9 20.2 %fusion.6 = (f32[1024]{0:T(1024)S(1)}, f32[1024]{0:T(1024)S(1)}, f32[1024]{0:T(1024)S(1)}, f32[2048,1024]{0,1:T(8,128)}) fusion(f32[1024]{0:T(1024)S(1)} %log_add_fusion.2, f32[1024,2048]{1,0:T(8,128)} %get-tuple-element.37, pred[1024,1024]{1,0:T(32,128)(4,1)S(1)} %broadcast_compare_fusion, pred[]{:T(512)S(6)} %gt.3, f32[2048,1024]{0,1:T(8,128)} %fusion.68, ...), kind=kOutput, calls=%fused_computation.18 | convolution fusion | flops 569373696 | bytes 53239808 | tf_op jit(solution)/shard_map/dot_general | solution.py:33
  139.1 12.5 %multiply_convert_fusion.2 = (bf16[1024,2048]{1,0:T(8,128)(2,1)S(1)}, bf16[1024,2048]{1,0:T(8,128)(2,1)S(1)}, bf16[1024,2048]{1,0:T(8,128)(2,1)S(1)}, bf16[1024,2048]{1,0:T(8,128)(2,1)S(1)}) fusion(f32[1024]{0:T(1024)S(1)} %select_reduce_fusion, f32[1024]{0:T(1024)S(1)} %log_add_fusion.2, f32[1024,2048]{1,0:T(8,128)} %get-tuple-element.37, ...), kind=kLoop, calls=%fused_computation.26 | loop fusion | flops 33554432 | bytes 51400704 | tf_op jit(solution)/shard_map/convert_element_type | solution.py:58
  157.2 2.6 fusion.47
  159.8 3.3 fusion.38
  163.1 2.5 fusion.53
  165.6 2.5 fusion.44
  168.2 4.9 multiply_convert_fusion.1
  173.1 3.2 fusion.50
  176.2 3.5 fusion.56
  179.7 2.3 fusion.58
  182.0 2.2 fusion.57
  185.2 4.3 all-to-all-start.4
  189.6 2.8 pad_maximum_fusion
  198.8 2.2 fusion.20
  201.0 2.5 fusion.41
  209.0 2.6 reshape.278
  211.6 21.7 %collective-permute-done.2 = f32[1024,384]{1,0:T(8,128)} collective-permute-done((f32[1024,384]{1,0:T(8,128)}, f32[1024,384]{1,0:T(8,128)}, u32[]{:S(2)}, u32[]{:S(2)}) %collective-permute-start.2) | collective-permute-done | bytes 1572896 | tf_op jit(solution)/shard_map/ppermute | solution.py:14
  233.3 2.6 fusion.36
  235.9 5.6 all-to-all-start.5
  241.5 2.7 multiply_convert_fusion.4
  244.2 19.0 %collective-permute-done.3 = f32[1024,384]{0,1:T(8,128)} collective-permute-done((f32[1024,384]{0,1:T(8,128)}, f32[1024,384]{0,1:T(8,128)}, u32[]{:S(2)}, u32[]{:S(2)}) %collective-permute-start.3) | collective-permute-done | bytes 1572896 | tf_op jit(solution)/shard_map/ppermute | solution.py:14
  263.2 2.9 copy_bitcast_fusion
  266.1 10.1 all-to-all-done.5
  276.2 4.2 all-to-all-start.6
  288.2 5.7 all-to-all-done.6
  293.9 2.3 copy.94
  296.2 37.5 %reduce-scatter.4.cloned.1.call-done = f32[1536,2]{1,0:T(8,128)} async-done(((f32[3072,2]{1,0:T(8,128)}), f32[1536,2]{1,0:T(8,128)}) %reduce-scatter.4.cloned.1.call-update) | async-done | bytes 12304
  335.0 688.9 %psum.8 = f32[2,1536]{1,0:T(2,128)} all-reduce(f32[2,1536]{1,0:T(2,128)S(1)} %copy.105), channel_id=1, replica_groups=mesh['span'=16,'sp'=8,'fsdp'=2] {'span','sp'}, use_global_device_ids=true, to_apply=%region_16.17 | all-reduce | flops 3072 | bytes 24576 | tf_op jit(solution)/shard_map/psum | solution.py:154
  (98 shorter events, 35.1 us)
Async XLA Ops:
  7.2 10.0 copy-start.7
  9.5 16.7 %all-to-all-start.2 = ((bf16[128,8,384]{0,2,1:T(8,128)(2,1)}), bf16[128,8,384]{0,2,1:T(8,128)(2,1)}, u32[]{:S(2)}, u32[]{:S(2)}) async-start(bf16[128,8,384]{0,2,1:T(8,128)(2,1)} %bitcast.7), calls=%async_computation.2 | async-start | bytes 1572864 | tf_op jit(solution)/shard_map/all_to_all | solution.py:80
  17.2 28.6 %copy-start.5 = (bf16[1,128,3072]{2,1,0:T(8,128)(2,1)S(1)}, bf16[1,128,3072]{2,1,0:T(8,128)(2,1)}, u32[]{:S(2)}) copy-start(bf16[1,128,3072]{2,1,0:T(8,128)(2,1)} %param.7) | copy-start | bytes 2359300
  26.2 15.2 %all-to-all-start.1 = ((bf16[128,8,384]{2,0,1:T(8,128)(2,1)}), bf16[128,8,384]{2,0,1:T(8,128)(2,1)S(1)}, u32[]{:S(2)}, u32[]{:S(2)}) async-start(bf16[128,8,384]{2,0,1:T(8,128)(2,1)} %multiply_convert_fusion.5), calls=%async_computation.1 | async-start | bytes 1572864 | tf_op jit(solution)/shard_map/all_to_all | solution.py:79
  41.5 22.9 %copy-start.20 = (s32[1,32]{1,0:T(1,128)S(1)}, s32[1,32]{1,0:T(1,128)}, u32[]{:S(2)}) copy-start(s32[1,32]{1,0:T(1,128)} %param.13) | copy-start | bytes 388
  41.5 22.9 %copy-start.19 = (s32[1,1024]{1,0:T(1,128)S(1)}, s32[1,1024]{1,0:T(1,128)}, u32[]{:S(2)}) copy-start(s32[1,1024]{1,0:T(1,128)} %param.12) | copy-start | bytes 12292
  41.5 18.7 %all-to-all-start.3 = ((bf16[128,8,384]{0,2,1:T(8,128)(2,1)}), bf16[128,8,384]{0,2,1:T(8,128)(2,1)}, u32[]{:S(2)}, u32[]{:S(2)}) async-start(bf16[128,8,384]{0,2,1:T(8,128)(2,1)} %bitcast.118), calls=%async_computation.3 | async-start | bytes 1572864 | tf_op jit(solution)/shard_map/all_to_all | solution.py:81
  46.0 6.1 copy-start.2
  46.3 39.1 %collective-permute-start = (bf16[1024,384]{1,0:T(8,128)(2,1)S(1)}, bf16[1024,384]{1,0:T(8,128)(2,1)}, u32[]{:S(2)}, u32[]{:S(2)}) collective-permute-start(bf16[1024,384]{1,0:T(8,128)(2,1)S(1)} %bitcast.91), channel_id=1, source_target_pairs={{0,16},{16,32},{32,48},{48,64},{64,80},{80,96},{96,112},{112,128},... | collective-permute-start | bytes 2359304 | tf_op jit(solution)/shard_map/ppermute | solution.py:14
  60.1 25.3 %all-to-all-start = ((bf16[128,8,384]{2,0,1:T(8,128)(2,1)}), bf16[128,8,384]{2,0,1:T(8,128)(2,1)}, u32[]{:S(2)}, u32[]{:S(2)}) async-start(bf16[128,8,384]{2,0,1:T(8,128)(2,1)} %multiply_convert_fusion.6), calls=%async_computation | async-start | bytes 1572864 | tf_op jit(solution)/shard_map/all_to_all | solution.py:78
  69.7 38.3 %collective-permute-start.1 = (bf16[1024,384]{1,0:T(8,128)(2,1)}, bf16[1024,384]{1,0:T(8,128)(2,1)}, u32[]{:S(2)}, u32[]{:S(2)}) collective-permute-start(bf16[1024,384]{1,0:T(8,128)(2,1)} %bitcast.102), channel_id=1, source_target_pairs={{0,16},{16,32},{32,48},{48,64},{64,80},{80,96},{96,112},{112,128},... | collective-permute-start | bytes 2359304 | tf_op jit(solution)/shard_map/ppermute | solution.py:14
  87.7 11.7 %copy-start.1 = (f32[1024,2048]{1,0:T(8,128)}, f32[1024,2048]{1,0:T(8,128)S(1)}, u32[]{:S(2)}) copy-start(f32[1024,2048]{1,0:T(8,128)S(1)} %fusion.75) | copy-start | bytes 25165828
  90.4 9.0 copy-start
  99.4 8.6 copy-start.4
  99.4 8.6 copy-start.13
  139.1 12.6 %copy-start.14 = (bf16[8,128,384]{2,1,0:T(8,128)(2,1)S(1)}, bf16[8,128,384]{2,1,0:T(8,128)(2,1)}, u32[]{:S(2)}) copy-start(bf16[8,128,384]{2,1,0:T(8,128)(2,1)} %copy.81) | copy-start | bytes 2359300
  151.6 5.6 copy-start.9
  153.3 14.8 %slice-start.2 = ((s8[8388608]{0:T(1024)(128)(4,1)}), s8[4194304]{0:T(1024)(128)(4,1)S(1)}, s32[]{:S(2)}) async-start(s8[8388608]{0:T(1024)(128)(4,1)} %bitcast.89), calls=%async_computation.11 | async-start | bytes 8388608
  155.9 12.2 %slice-start = ((s8[8388608]{0:T(1024)(128)(4,1)}), s8[4194304]{0:T(1024)(128)(4,1)S(1)}, s32[]{:S(2)}) async-start(s8[8388608]{0:T(1024)(128)(4,1)} %bitcast.87), calls=%async_computation.9 | async-start | bytes 8388608
  157.2 10.9 %slice-start.3 = ((s8[8388608]{0:T(1024)(128)(4,1)}), s8[4194304]{0:T(1024)(128)(4,1)S(1)}, s32[]{:S(2)}) async-start(s8[8388608]{0:T(1024)(128)(4,1)} %bitcast.89), calls=%async_computation.12 | async-start | bytes 8388608
  159.8 8.3 slice-start.1
  179.7 2.4 copy-start.10
  185.2 10.5 %copy-start.17 = (f32[1024,128]{0,1:T(8,128)S(1)}, f32[1024,128]{0,1:T(8,128)}, u32[]{:S(2)}) copy-start(f32[1024,128]{0,1:T(8,128)} %fusion.16) | copy-start | bytes 1572868
  185.2 10.5 %copy-start.18 = (f32[1024,128]{0,1:T(8,128)S(1)}, f32[1024,128]{0,1:T(8,128)}, u32[]{:S(2)}) copy-start(f32[1024,128]{0,1:T(8,128)} %fusion.12) | copy-start | bytes 1572868
  185.2 18.3 %all-to-all-start.4 = ((bf16[8,128,384]{2,1,0:T(8,128)(2,1)}), bf16[8,128,384]{2,1,0:T(8,128)(2,1)}, u32[]{:S(2)}, u32[]{:S(2)}) async-start(bf16[8,128,384]{2,1,0:T(8,128)(2,1)} %pad_maximum_fusion.2), calls=%async_computation.4 | async-start | bytes 1572864 | tf_op jit(solution)/shard_map/all_to_all | solution.py:141
  189.6 9.2 copy-start.12
  192.4 41.0 %collective-permute-start.2 = (f32[1024,384]{1,0:T(8,128)}, f32[1024,384]{1,0:T(8,128)}, u32[]{:S(2)}, u32[]{:S(2)}) collective-permute-start(f32[1024,384]{1,0:T(8,128)} %pad_maximum_fusion), channel_id=1, source_target_pairs={{16,0},{32,16},{48,32},{64,48},{80,64},{96,80},{112,96},{128,112},... | collective-permute-start | bytes 4718600 | tf_op jit(solution)/shard_map/ppermute | solution.py:14
  195.8 5.3 copy-start.11
  197.0 6.5 copy-start.3
  197.0 66.2 %collective-permute-start.3 = (f32[1024,384]{0,1:T(8,128)}, f32[1024,384]{0,1:T(8,128)}, u32[]{:S(2)}, u32[]{:S(2)}) collective-permute-start(f32[1024,384]{0,1:T(8,128)} %pad_maximum_fusion.1), channel_id=1, source_target_pairs={{16,0},{32,16},{48,32},{64,48},{80,64},{96,80},{112,96},{128,112},... | collective-permute-start | bytes 4718600 | tf_op jit(solution)/shard_map/ppermute | solution.py:14
  205.6 27.8 %copy-start.15 = (f32[1024,128]{1,0:T(8,128)S(1)}, f32[1024,128]{1,0:T(8,128)}, u32[]{:S(2)}) copy-start(f32[1024,128]{1,0:T(8,128)} %fusion.38) | copy-start | bytes 1572868
  205.6 27.7 %copy-start.16 = (f32[1024,128]{1,0:T(8,128)S(1)}, f32[1024,128]{1,0:T(8,128)}, u32[]{:S(2)}) copy-start(f32[1024,128]{1,0:T(8,128)} %fusion.44) | copy-start | bytes 1572868
  209.0 32.5 %copy-start.6 = (bf16[1,128,3072]{2,1,0:T(8,128)(2,1)S(1)}, bf16[1,128,3072]{2,1,0:T(8,128)(2,1)}, u32[]{:S(2)}) copy-start(bf16[1,128,3072]{2,1,0:T(8,128)(2,1)} %param.7) | copy-start | bytes 2359300
  235.9 40.3 %all-to-all-start.5 = ((bf16[8,128,384]{2,1,0:T(8,128)(2,1)}), bf16[8,128,384]{2,1,0:T(8,128)(2,1)S(1)}, u32[]{:S(2)}, u32[]{:S(2)}) async-start(bf16[8,128,384]{2,1,0:T(8,128)(2,1)} %bitcast.119), calls=%async_computation.5 | async-start | bytes 1572864 | tf_op jit(solution)/shard_map/all_to_all | solution.py:144
  276.2 17.6 %all-to-all-start.6 = ((bf16[8,128,384]{1,2,0:T(8,128)(2,1)}), bf16[8,128,384]{1,2,0:T(8,128)(2,1)}, u32[]{:S(2)}, u32[]{:S(2)}) async-start(bf16[8,128,384]{1,2,0:T(8,128)(2,1)} %copy_bitcast_fusion), calls=%async_computation.6 | async-start | bytes 1572864 | tf_op jit(solution)/shard_map/all_to_all | solution.py:147
  280.5 53.2 %reduce-scatter.4.cloned.1.call-start = ((), (), s32[]{:S(2)}) async-start(), calls=%async_computation.8 | async-start | bytes 2359296
  281.5 5.3 copy-start.8
Sparse Core Ops, SparseCore 0:
  287.0 46.5 reduce-scatter.3
where the time goes:
time: 1040 us; the launch traced here: 1030 us
  blocking collectives  691 us (66%)
  waiting for transfers between devices  130 us (12%)
  matrix products  79.4 us (8%)
  other arithmetic  48.8 us (5%)
  starting transfers between devices  42.3 us (4%)
  local copies, waits for them, and re-layouts  24.5 us (2%)
  between operations  14.8 us (1%)
    psum x1, blocking collectives, on_device(): summed = lax.psum(partial_value, ('span', 'sp'))  689 us
    dot_general x6, matrix products, across(): lax.dot_general(left, right, (((1,), (1,)), ((), ())), preferred_element_...  45 us
    ppermute x4, waiting for transfers between devices, from_behind(): lax.ppermute(value, axis, [(source, source + steps) for source in range(f...  40.7 us
    unnamed x2, waiting for transfers between devices  37.5 us
    dot_general x12, matrix products, downward(): lax.dot_general(left, right, (((0,), (0,)), ((), ())), preferred_element_...  26.4 us
  transfers between devices with their start and end apart: 12, of which 9 were waited for; matrix products, arithmetic and copies ran while one was open for 7% of the time, Pallas kernels for 0%

commit v1 on v0

--- a/solution.py
+++ b/solution.py
@@ -151,7 +151,8 @@
     query_back, query_gain = norm_backward(query_tokens, q_normal, q_inverse, gain_full[0])
     key_back_rows, key_gain = norm_backward(key_tokens, k_normal, k_inverse, gain_full[1])
     partial_value = jnp.stack([query_gain, key_gain])
-    summed = lax.psum(partial_value, ("span", "sp"))
+    half = lax.psum(partial_value, "sp")
+    summed = lax.psum(half, "span")
     gain_grad = lax.psum_scatter(summed, "fsdp", scatter_dimension=1, tiled=True)
     return (query_back[None], key_back_rows[None], value_tokens[None], gain_grad)
 

time: 1040 us -> 460 us (0.44)
  blocking collectives: 691 us -> 113 us
    psum x1 -> x2, blocking collectives: 689 us -> 111 us  [the longest x1 77.2 us: on_device(): summed = lax.psum(half, 'span')]
  transfers between devices with their start and end apart: 12 -> 12, of which waited for: 9 -> 9; matrix products, arithmetic and copies ran while one was open for 7% -> 16% of each run, Pallas kernels for 0% -> 0%
where the time goes in v1:
time: 460 us; the launch traced here: 453 us
  waiting for transfers between devices  130 us (28%)
  blocking collectives  113 us (25%)
  matrix products  79.4 us (17%)
  other arithmetic  48.8 us (11%)
  starting transfers between devices  42.3 us (9%)
  local copies, waits for them, and re-layouts  24.5 us (5%)
  between operations  14.8 us (3%)
    psum x1, blocking collectives, on_device(): summed = lax.psum(half, 'span')  77.2 us
    dot_general x6, matrix products, across(): lax.dot_general(left, right, (((1,), (1,)), ((), ())), preferred_element_...  45 us
    ppermute x4, waiting for transfers between devices, from_behind(): lax.ppermute(value, axis, [(source, source + steps) for source in range(f...  40.7 us
    unnamed x2, waiting for transfers between devices  37.5 us
    psum x1, blocking collectives, on_device(): half = lax.psum(partial_value, 'sp')  34 us
    dot_general x12, matrix products, downward(): lax.dot_general(left, right, (((0,), (0,)), ((), ())), preferred_element_...  26.4 us
    convert_element_type x2, other arithmetic, head_grads(): weights = (factor * probs).astype(jnp.bfloat16)  17.4 us
    all_to_all x1, waiting for transfers between devices, on_device(): lax.all_to_all(q_ready, 'sp', split_axis=1, concat_axis=0, tiled=True)  12.8 us
  transfers between devices with their start and end apart: 12, of which 9 were waited for; matrix products, arithmetic and copies ran while one was open for 16% of the time, Pallas kernels for 0%

profile of v1, /device:TPU:0, one launch (start us, length us, event | category | flops | bytes accessed | tf_op | source)
XLA Modules:
  0.0 453.3 jit_solution(6179762665885015336)
XLA Ops:
  7.2 2.4 copy.78
  9.5 4.2 all-to-all-start.2
  18.8 7.4 %all-to-all-done.2 = bf16[128,8,384]{0,2,1:T(8,128)(2,1)} async-done(((bf16[128,8,384]{0,2,1:T(8,128)(2,1)}), bf16[128,8,384]{0,2,1:T(8,128)(2,1)}, u32[]{:S(2)}, u32[]{:S(2)}) %all-to-all-start.2) | async-done | bytes 786464 | tf_op jit(solution)/shard_map/all_to_all | solution.py:80
  26.2 3.5 all-to-all-start.1
  29.8 2.3 copy.80
  32.1 9.4 %all-to-all-done.1 = bf16[128,8,384]{2,0,1:T(8,128)(2,1)S(1)} async-done(((bf16[128,8,384]{2,0,1:T(8,128)(2,1)}), bf16[128,8,384]{2,0,1:T(8,128)(2,1)S(1)}, u32[]{:S(2)}, u32[]{:S(2)}) %all-to-all-start.1) | async-done | bytes 786464 | tf_op jit(solution)/shard_map/all_to_all | solution.py:79
  41.5 4.3 all-to-all-start.3
  46.3 5.9 %collective-permute-start = (bf16[1024,384]{1,0:T(8,128)(2,1)S(1)}, bf16[1024,384]{1,0:T(8,128)(2,1)}, u32[]{:S(2)}, u32[]{:S(2)}) collective-permute-start(bf16[1024,384]{1,0:T(8,128)(2,1)S(1)} %bitcast.91), channel_id=1, source_target_pairs={{0,16},{16,32},{32,48},{48,64},{64,80},{80,96},{96,112},{112,128},... | collective-permute-start | bytes 2359304 | tf_op jit(solution)/shard_map/ppermute | solution.py:14
  53.5 6.6 %all-to-all-done.3 = bf16[128,8,384]{0,2,1:T(8,128)(2,1)} async-done(((bf16[128,8,384]{0,2,1:T(8,128)(2,1)}), bf16[128,8,384]{0,2,1:T(8,128)(2,1)}, u32[]{:S(2)}, u32[]{:S(2)}) %all-to-all-start.3) | async-done | bytes 786464 | tf_op jit(solution)/shard_map/all_to_all | solution.py:81
  60.1 4.2 all-to-all-start
  65.1 2.3 copy.79
  67.4 2.3 copy.81
  69.7 2.9 collective-permute-start.1
  72.6 12.8 %all-to-all-done = bf16[128,8,384]{2,0,1:T(8,128)(2,1)} async-done(((bf16[128,8,384]{2,0,1:T(8,128)(2,1)}), bf16[128,8,384]{2,0,1:T(8,128)(2,1)}, u32[]{:S(2)}, u32[]{:S(2)}) %all-to-all-start) | async-done | bytes 786464 | tf_op jit(solution)/shard_map/all_to_all | solution.py:78
  85.4 2.3 fusion.75
  87.7 2.7 fusion.82
  90.4 9.0 %fusion.9 = (f32[1024]{0:T(1024)S(1)}, f32[1024]{0:T(1024)S(1)}, f32[1024]{0:T(1024)S(1)}, f32[1024,2048]{1,0:T(8,128)}) fusion(pred[1024,1024]{1,0:T(32,128)(4,1)S(1)} %broadcast_compare_fusion, pred[]{:T(512)S(6)} %gt.3, f32[1024,2048]{1,0:T(8,128)S(1)} %fusion.82, f32[1024,2048]{1,0:T(8,128)S(1)} %fusion.75, bf16[1024,384]{1,0:T(8,128)(2,1)S(1)} %bitcast.94, ...), kind=kOutput, calls=%fused_computation.27 | convolution fusion | flops 556790784 | bytes 28061696 | tf_op jit(solution)/shard_map/dot_general | solution.py:33
  99.4 8.6 %exponential_reduce_fusion.2 = (f32[1024]{0:T(1024)S(1)}, f32[1024]{0:T(1024)S(1)}, f32[1024]{0:T(1024)S(1)}) fusion(f32[1024,2048]{1,0:T(8,128)} %get-tuple-element.37, pred[1024,1024]{1,0:T(32,128)(4,1)S(1)} %broadcast_compare_fusion, pred[]{:T(512)S(6)} %gt.3, f32[1024]{0:T(1024)S(1)} %get-tuple-element.22, f32[1024]{0:T(1024)S(1)} %get-tuple-element.24, ...), kind=kLoop, calls=%fused_computation.23 | loop fusion | flops 25162752 | bytes 26238976 | tf_op jit(solution)/shard_map/reduce_sum | solution.py:51
  108.0 5.4 %fusion.68 = f32[2048,1024]{0,1:T(8,128)} fusion(bf16[1024,384]{1,0:T(8,128)(2,1)} %collective-permute-done.1, bf16[1024,384]{1,0:T(8,128)(2,1)S(1)} %bitcast.104, bf16[1024,384]{1,0:T(8,128)(2,1)S(1)} %bitcast.112), kind=kOutput, calls=%fused_computation.105 | convolution fusion | flops 537919488 | bytes 10223616 | tf_op jit(solution)/shard_map/dot_general | solution.py:33
  113.4 5.4 %fusion.61 = f32[2048,1024]{0,1:T(8,128)} fusion(bf16[1024,384]{1,0:T(8,128)(2,1)S(1)} %bitcast.105, bf16[1024,384]{1,0:T(8,128)(2,1)} %collective-permute-done.1, bf16[1024,384]{1,0:T(8,128)(2,1)S(1)} %bitcast.113), kind=kOutput, calls=%fused_computation.99 | convolution fusion | flops 537919488 | bytes 10223616 | tf_op jit(solution)/shard_map/dot_general | solution.py:33
  118.9 20.2 %fusion.6 = (f32[1024]{0:T(1024)S(1)}, f32[1024]{0:T(1024)S(1)}, f32[1024]{0:T(1024)S(1)}, f32[2048,1024]{0,1:T(8,128)}) fusion(f32[1024]{0:T(1024)S(1)} %log_add_fusion.2, f32[1024,2048]{1,0:T(8,128)} %get-tuple-element.37, pred[1024,1024]{1,0:T(32,128)(4,1)S(1)} %broadcast_compare_fusion, pred[]{:T(512)S(6)} %gt.3, f32[2048,1024]{0,1:T(8,128)} %fusion.68, ...), kind=kOutput, calls=%fused_computation.18 | convolution fusion | flops 569373696 | bytes 53239808 | tf_op jit(solution)/shard_map/dot_general | solution.py:33
  139.1 12.5 %multiply_convert_fusion.2 = (bf16[1024,2048]{1,0:T(8,128)(2,1)S(1)}, bf16[1024,2048]{1,0:T(8,128)(2,1)S(1)}, bf16[1024,2048]{1,0:T(8,128)(2,1)S(1)}, bf16[1024,2048]{1,0:T(8,128)(2,1)S(1)}) fusion(f32[1024]{0:T(1024)S(1)} %select_reduce_fusion, f32[1024]{0:T(1024)S(1)} %log_add_fusion.2, f32[1024,2048]{1,0:T(8,128)} %get-tuple-element.37, ...), kind=kLoop, calls=%fused_computation.26 | loop fusion | flops 33554432 | bytes 51400704 | tf_op jit(solution)/shard_map/convert_element_type | solution.py:58
  157.2 2.6 fusion.47
  159.8 3.3 fusion.38
  163.1 2.5 fusion.53
  165.6 2.5 fusion.44
  168.2 4.9 %multiply_convert_fusion.1 = (bf16[1024,2048]{1,0:T(8,128)(2,1)}, bf16[1024,2048]{1,0:T(8,128)(2,1)}) fusion(f32[1024]{0:T(1024)S(1)} %select_reduce_fusion, f32[1024]{0:T(1024)S(1)} %get-tuple-element.40, f32[1024,2048]{1,0:T(8,128)S(1)} %bitcast.88, pred[1024,1024]{1,0:T(32,128)(4,1)S(1)} %broadcast_compare_fusion, pred[]{:T(512)S(6)} %gt.3, ...), kind=kLoop, calls=%fused_computation.25 | loop fusion | flops 16777216 | bytes 26226688 | tf_op jit(solution)/shard_map/convert_element_type | solution.py:58
  173.1 3.2 fusion.50
  176.2 3.5 fusion.56
  179.7 2.3 fusion.58
  185.2 4.3 all-to-all-start.4
  189.6 2.8 pad_maximum_fusion
  198.8 2.2 fusion.20
  201.0 2.5 fusion.41
  209.0 2.6 reshape.278
  211.6 21.7 %collective-permute-done.2 = f32[1024,384]{1,0:T(8,128)} collective-permute-done((f32[1024,384]{1,0:T(8,128)}, f32[1024,384]{1,0:T(8,128)}, u32[]{:S(2)}, u32[]{:S(2)}) %collective-permute-start.2) | collective-permute-done | bytes 1572896 | tf_op jit(solution)/shard_map/ppermute | solution.py:14
  233.3 2.6 fusion.36
  235.9 5.6 %all-to-all-start.5 = ((bf16[8,128,384]{2,1,0:T(8,128)(2,1)}), bf16[8,128,384]{2,1,0:T(8,128)(2,1)S(1)}, u32[]{:S(2)}, u32[]{:S(2)}) async-start(bf16[8,128,384]{2,1,0:T(8,128)(2,1)} %bitcast.119), calls=%async_computation.5 | async-start | bytes 1572864 | tf_op jit(solution)/shard_map/all_to_all | solution.py:144
  241.5 2.7 multiply_convert_fusion.4
  244.2 19.0 %collective-permute-done.3 = f32[1024,384]{0,1:T(8,128)} collective-permute-done((f32[1024,384]{0,1:T(8,128)}, f32[1024,384]{0,1:T(8,128)}, u32[]{:S(2)}, u32[]{:S(2)}) %collective-permute-start.3) | collective-permute-done | bytes 1572896 | tf_op jit(solution)/shard_map/ppermute | solution.py:14
  263.2 2.9 copy_bitcast_fusion
  266.1 10.1 %all-to-all-done.5 = bf16[8,128,384]{2,1,0:T(8,128)(2,1)S(1)} async-done(((bf16[8,128,384]{2,1,0:T(8,128)(2,1)}), bf16[8,128,384]{2,1,0:T(8,128)(2,1)S(1)}, u32[]{:S(2)}, u32[]{:S(2)}) %all-to-all-start.5) | async-done | bytes 786464 | tf_op jit(solution)/shard_map/all_to_all | solution.py:144
  276.2 4.2 all-to-all-start.6
  288.2 5.7 %all-to-all-done.6 = bf16[8,128,384]{1,2,0:T(8,128)(2,1)} async-done(((bf16[8,128,384]{1,2,0:T(8,128)(2,1)}), bf16[8,128,384]{1,2,0:T(8,128)(2,1)}, u32[]{:S(2)}, u32[]{:S(2)}) %all-to-all-start.6) | async-done | bytes 786464 | tf_op jit(solution)/shard_map/all_to_all | solution.py:147
  293.9 2.3 copy.94
  296.2 37.5 %reduce-scatter.4.cloned.1.call-done = f32[1536,2]{1,0:T(8,128)} async-done(((f32[3072,2]{1,0:T(8,128)}), f32[1536,2]{1,0:T(8,128)}) %reduce-scatter.4.cloned.1.call-update) | async-done | bytes 12304
  335.0 34.0 %psum.17 = f32[2,1536]{1,0:T(2,128)S(1)} all-reduce(f32[2,1536]{1,0:T(2,128)S(1)} %copy.105), channel_id=1, replica_groups=mesh['span'=16,'sp'=8,'fsdp'=2] {'sp'}, use_global_device_ids=true, to_apply=%region_16.17 | all-reduce | flops 3072 | bytes 24576 | tf_op jit(solution)/shard_map/psum | solution.py:154
  369.1 77.2 %psum.16 = f32[2,1536]{1,0:T(2,128)} all-reduce(f32[2,1536]{1,0:T(2,128)S(1)} %psum.17), channel_id=1, replica_groups=mesh['span'=16,'sp'=8,'fsdp'=2] {'span'}, use_global_device_ids=true, to_apply=%region_17.18 | all-reduce | flops 3072 | bytes 24576 | tf_op jit(solution)/shard_map/psum | solution.py:155
  (99 shorter events, 37.3 us)
Async XLA Ops:
  7.2 10.0 %copy-start.7 = (bf16[1,128,3072]{2,1,0:T(8,128)(2,1)S(1)}, bf16[1,128,3072]{2,1,0:T(8,128)(2,1)}, u32[]{:S(2)}) copy-start(bf16[1,128,3072]{2,1,0:T(8,128)(2,1)} %param.8) | copy-start | bytes 2359300
  9.5 16.7 %all-to-all-start.2 = ((bf16[128,8,384]{0,2,1:T(8,128)(2,1)}), bf16[128,8,384]{0,2,1:T(8,128)(2,1)}, u32[]{:S(2)}, u32[]{:S(2)}) async-start(bf16[128,8,384]{0,2,1:T(8,128)(2,1)} %bitcast.7), calls=%async_computation.2 | async-start | bytes 1572864 | tf_op jit(solution)/shard_map/all_to_all | solution.py:80
  17.2 28.6 %copy-start.5 = (bf16[1,128,3072]{2,1,0:T(8,128)(2,1)S(1)}, bf16[1,128,3072]{2,1,0:T(8,128)(2,1)}, u32[]{:S(2)}) copy-start(bf16[1,128,3072]{2,1,0:T(8,128)(2,1)} %param.7) | copy-start | bytes 2359300
  26.2 15.2 %all-to-all-start.1 = ((bf16[128,8,384]{2,0,1:T(8,128)(2,1)}), bf16[128,8,384]{2,0,1:T(8,128)(2,1)S(1)}, u32[]{:S(2)}, u32[]{:S(2)}) async-start(bf16[128,8,384]{2,0,1:T(8,128)(2,1)} %multiply_convert_fusion.5), calls=%async_computation.1 | async-start | bytes 1572864 | tf_op jit(solution)/shard_map/all_to_all | solution.py:79
  41.5 22.9 %copy-start.20 = (s32[1,32]{1,0:T(1,128)S(1)}, s32[1,32]{1,0:T(1,128)}, u32[]{:S(2)}) copy-start(s32[1,32]{1,0:T(1,128)} %param.13) | copy-start | bytes 388
  41.5 22.9 %copy-start.19 = (s32[1,1024]{1,0:T(1,128)S(1)}, s32[1,1024]{1,0:T(1,128)}, u32[]{:S(2)}) copy-start(s32[1,1024]{1,0:T(1,128)} %param.12) | copy-start | bytes 12292
  41.5 18.7 %all-to-all-start.3 = ((bf16[128,8,384]{0,2,1:T(8,128)(2,1)}), bf16[128,8,384]{0,2,1:T(8,128)(2,1)}, u32[]{:S(2)}, u32[]{:S(2)}) async-start(bf16[128,8,384]{0,2,1:T(8,128)(2,1)} %bitcast.118), calls=%async_computation.3 | async-start | bytes 1572864 | tf_op jit(solution)/shard_map/all_to_all | solution.py:81
  46.0 6.1 %copy-start.2 = (f32[16,8,8,384]{3,2,1,0:T(8,128)}, f32[16,8,8,384]{3,2,1,0:T(8,128)S(1)}, u32[]{:S(2)}) copy-start(f32[16,8,8,384]{3,2,1,0:T(8,128)S(1)} %copy.107) | copy-start | bytes 4718596
  46.3 39.1 %collective-permute-start = (bf16[1024,384]{1,0:T(8,128)(2,1)S(1)}, bf16[1024,384]{1,0:T(8,128)(2,1)}, u32[]{:S(2)}, u32[]{:S(2)}) collective-permute-start(bf16[1024,384]{1,0:T(8,128)(2,1)S(1)} %bitcast.91), channel_id=1, source_target_pairs={{0,16},{16,32},{32,48},{48,64},{64,80},{80,96},{96,112},{112,128},... | collective-permute-start | bytes 2359304 | tf_op jit(solution)/shard_map/ppermute | solution.py:14
  60.1 25.3 %all-to-all-start = ((bf16[128,8,384]{2,0,1:T(8,128)(2,1)}), bf16[128,8,384]{2,0,1:T(8,128)(2,1)}, u32[]{:S(2)}, u32[]{:S(2)}) async-start(bf16[128,8,384]{2,0,1:T(8,128)(2,1)} %multiply_convert_fusion.6), calls=%async_computation | async-start | bytes 1572864 | tf_op jit(solution)/shard_map/all_to_all | solution.py:78
  69.7 38.3 %collective-permute-start.1 = (bf16[1024,384]{1,0:T(8,128)(2,1)}, bf16[1024,384]{1,0:T(8,128)(2,1)}, u32[]{:S(2)}, u32[]{:S(2)}) collective-permute-start(bf16[1024,384]{1,0:T(8,128)(2,1)} %bitcast.102), channel_id=1, source_target_pairs={{0,16},{16,32},{32,48},{48,64},{64,80},{80,96},{96,112},{112,128},... | collective-permute-start | bytes 2359304 | tf_op jit(solution)/shard_map/ppermute | solution.py:14
  87.7 11.7 %copy-start.1 = (f32[1024,2048]{1,0:T(8,128)}, f32[1024,2048]{1,0:T(8,128)S(1)}, u32[]{:S(2)}) copy-start(f32[1024,2048]{1,0:T(8,128)S(1)} %fusion.75) | copy-start | bytes 25165828
  90.4 9.0 %copy-start = (f32[1024,2048]{1,0:T(8,128)}, f32[1024,2048]{1,0:T(8,128)S(1)}, u32[]{:S(2)}) copy-start(f32[1024,2048]{1,0:T(8,128)S(1)} %fusion.82) | copy-start | bytes 25165828
  99.4 8.6 %copy-start.4 = (bf16[8,128,384]{2,1,0:T(8,128)(2,1)S(1)}, bf16[8,128,384]{2,1,0:T(8,128)(2,1)}, u32[]{:S(2)}) copy-start(bf16[8,128,384]{2,1,0:T(8,128)(2,1)} %copy.79) | copy-start | bytes 2359300
  99.4 8.6 %copy-start.13 = (bf16[8,128,384]{2,1,0:T(8,128)(2,1)S(1)}, bf16[8,128,384]{2,1,0:T(8,128)(2,1)}, u32[]{:S(2)}) copy-start(bf16[8,128,384]{2,1,0:T(8,128)(2,1)} %copy.81) | copy-start | bytes 2359300
  139.1 12.6 %copy-start.14 = (bf16[8,128,384]{2,1,0:T(8,128)(2,1)S(1)}, bf16[8,128,384]{2,1,0:T(8,128)(2,1)}, u32[]{:S(2)}) copy-start(bf16[8,128,384]{2,1,0:T(8,128)(2,1)} %copy.81) | copy-start | bytes 2359300
  151.6 5.6 %copy-start.9 = (bf16[1024,2048]{1,0:T(8,128)(2,1)}, bf16[1024,2048]{1,0:T(8,128)(2,1)S(1)}, u32[]{:S(2)}) copy-start(bf16[1024,2048]{1,0:T(8,128)(2,1)S(1)} %get-tuple-element.28) | copy-start | bytes 12582916
  153.3 14.8 %slice-start.2 = ((s8[8388608]{0:T(1024)(128)(4,1)}), s8[4194304]{0:T(1024)(128)(4,1)S(1)}, s32[]{:S(2)}) async-start(s8[8388608]{0:T(1024)(128)(4,1)} %bitcast.89), calls=%async_computation.11 | async-start | bytes 8388608
  155.9 12.2 %slice-start = ((s8[8388608]{0:T(1024)(128)(4,1)}), s8[4194304]{0:T(1024)(128)(4,1)S(1)}, s32[]{:S(2)}) async-start(s8[8388608]{0:T(1024)(128)(4,1)} %bitcast.87), calls=%async_computation.9 | async-start | bytes 8388608
  157.2 10.9 %slice-start.3 = ((s8[8388608]{0:T(1024)(128)(4,1)}), s8[4194304]{0:T(1024)(128)(4,1)S(1)}, s32[]{:S(2)}) async-start(s8[8388608]{0:T(1024)(128)(4,1)} %bitcast.89), calls=%async_computation.12 | async-start | bytes 8388608
  159.8 8.3 %slice-start.1 = ((s8[8388608]{0:T(1024)(128)(4,1)}), s8[4194304]{0:T(1024)(128)(4,1)S(1)}, s32[]{:S(2)}) async-start(s8[8388608]{0:T(1024)(128)(4,1)} %bitcast.87), calls=%async_computation.10 | async-start | bytes 8388608
  179.7 2.4 copy-start.10
  185.2 10.5 %copy-start.17 = (f32[1024,128]{0,1:T(8,128)S(1)}, f32[1024,128]{0,1:T(8,128)}, u32[]{:S(2)}) copy-start(f32[1024,128]{0,1:T(8,128)} %fusion.16) | copy-start | bytes 1572868
  185.2 10.5 %copy-start.18 = (f32[1024,128]{0,1:T(8,128)S(1)}, f32[1024,128]{0,1:T(8,128)}, u32[]{:S(2)}) copy-start(f32[1024,128]{0,1:T(8,128)} %fusion.12) | copy-start | bytes 1572868
  185.2 18.3 %all-to-all-start.4 = ((bf16[8,128,384]{2,1,0:T(8,128)(2,1)}), bf16[8,128,384]{2,1,0:T(8,128)(2,1)}, u32[]{:S(2)}, u32[]{:S(2)}) async-start(bf16[8,128,384]{2,1,0:T(8,128)(2,1)} %pad_maximum_fusion.2), calls=%async_computation.4 | async-start | bytes 1572864 | tf_op jit(solution)/shard_map/all_to_all | solution.py:141
  189.6 9.2 %copy-start.12 = (bf16[1024,2048]{1,0:T(8,128)(2,1)S(1)}, bf16[1024,2048]{1,0:T(8,128)(2,1)}, u32[]{:S(2)}) copy-start(bf16[1024,2048]{1,0:T(8,128)(2,1)} %get-tuple-element.29) | copy-start | bytes 12582916
  192.4 41.0 %collective-permute-start.2 = (f32[1024,384]{1,0:T(8,128)}, f32[1024,384]{1,0:T(8,128)}, u32[]{:S(2)}, u32[]{:S(2)}) collective-permute-start(f32[1024,384]{1,0:T(8,128)} %pad_maximum_fusion), channel_id=1, source_target_pairs={{16,0},{32,16},{48,32},{64,48},{80,64},{96,80},{112,96},{128,112},... | collective-permute-start | bytes 4718600 | tf_op jit(solution)/shard_map/ppermute | solution.py:14
  195.8 5.3 %copy-start.11 = (bf16[1024,2048]{1,0:T(8,128)(2,1)S(1)}, bf16[1024,2048]{1,0:T(8,128)(2,1)}, u32[]{:S(2)}) copy-start(bf16[1024,2048]{1,0:T(8,128)(2,1)} %get-tuple-element.30) | copy-start | bytes 12582916
  197.0 6.5 %copy-start.3 = (f32[16,8,8,384]{3,2,1,0:T(8,128)S(1)}, f32[16,8,8,384]{3,2,1,0:T(8,128)}, u32[]{:S(2)}) copy-start(f32[16,8,8,384]{3,2,1,0:T(8,128)} %copy-done.2) | copy-start | bytes 4718596
  197.0 66.2 %collective-permute-start.3 = (f32[1024,384]{0,1:T(8,128)}, f32[1024,384]{0,1:T(8,128)}, u32[]{:S(2)}, u32[]{:S(2)}) collective-permute-start(f32[1024,384]{0,1:T(8,128)} %pad_maximum_fusion.1), channel_id=1, source_target_pairs={{16,0},{32,16},{48,32},{64,48},{80,64},{96,80},{112,96},{128,112},... | collective-permute-start | bytes 4718600 | tf_op jit(solution)/shard_map/ppermute | solution.py:14
  205.6 27.8 %copy-start.15 = (f32[1024,128]{1,0:T(8,128)S(1)}, f32[1024,128]{1,0:T(8,128)}, u32[]{:S(2)}) copy-start(f32[1024,128]{1,0:T(8,128)} %fusion.38) | copy-start | bytes 1572868
  205.6 27.7 %copy-start.16 = (f32[1024,128]{1,0:T(8,128)S(1)}, f32[1024,128]{1,0:T(8,128)}, u32[]{:S(2)}) copy-start(f32[1024,128]{1,0:T(8,128)} %fusion.44) | copy-start | bytes 1572868
  209.0 32.5 %copy-start.6 = (bf16[1,128,3072]{2,1,0:T(8,128)(2,1)S(1)}, bf16[1,128,3072]{2,1,0:T(8,128)(2,1)}, u32[]{:S(2)}) copy-start(bf16[1,128,3072]{2,1,0:T(8,128)(2,1)} %param.7) | copy-start | bytes 2359300
  235.9 40.3 %all-to-all-start.5 = ((bf16[8,128,384]{2,1,0:T(8,128)(2,1)}), bf16[8,128,384]{2,1,0:T(8,128)(2,1)S(1)}, u32[]{:S(2)}, u32[]{:S(2)}) async-start(bf16[8,128,384]{2,1,0:T(8,128)(2,1)} %bitcast.119), calls=%async_computation.5 | async-start | bytes 1572864 | tf_op jit(solution)/shard_map/all_to_all | solution.py:144
  276.2 17.6 %all-to-all-start.6 = ((bf16[8,128,384]{1,2,0:T(8,128)(2,1)}), bf16[8,128,384]{1,2,0:T(8,128)(2,1)}, u32[]{:S(2)}, u32[]{:S(2)}) async-start(bf16[8,128,384]{1,2,0:T(8,128)(2,1)} %copy_bitcast_fusion), calls=%async_computation.6 | async-start | bytes 1572864 | tf_op jit(solution)/shard_map/all_to_all | solution.py:147
  280.5 53.2 %reduce-scatter.4.cloned.1.call-start = ((), (), s32[]{:S(2)}) async-start(), calls=%async_computation.8 | async-start | bytes 2359296
  281.5 5.3 %copy-start.8 = (bf16[1,128,3072]{2,1,0:T(8,128)(2,1)S(1)}, bf16[1,128,3072]{2,1,0:T(8,128)(2,1)}, u32[]{:S(2)}) copy-start(bf16[1,128,3072]{2,1,0:T(8,128)(2,1)} %param.8) | copy-start | bytes 2359300
Sparse Core Ops, SparseCore 0:
  287.0 46.5 reduce-scatter.3
